TPU v7x, 32 devices: a whole 2x2x4 slice. The times are simulated.
32 devices in a mesh: section: 2 (over x), head: 4 (over y, core), tok: 4 (over z).
Axes of the slice: x: 2, y: 2, z: 4, core: 2. Of those that a mesh axis runs over, the one named last changes fastest.
Arguments:
- held_cotangents: bfloat16 [2, 2, 512, 2560], P('section', None, 'tok', 'head'), may hold values from -6 to 6
- entering_adjoint: bfloat16 [512, 2560], P('tok', 'head'), may hold values from -6 to 6
- saved_queries: bfloat16 [2, 512, 2560], P('section', 'tok', 'head'), may hold values from -1024 to 1024
- saved_keys: bfloat16 [2, 512, 2560], P('section', 'tok', 'head'), may hold values from -20 to 20
- value_weight: bfloat16 [2, 2560, 2560], P('section', None, 'head'), may hold values from -0.125 to 0.125
- out_weight: bfloat16 [2, 2560, 2560], P('section', 'tok', 'head'), may hold values from -0.125 to 0.125
- block_gate: float32 [2, 2560], P('section'), may hold values from -3 to 3
- time_gate: float32 [32, 2560], replicated, may hold values from -3 to 3
- timestep: int32 [1], replicated, may hold values from 0 to 31
Outputs:
- passed: bfloat16 [2, 2, 512, 2560], P('section', None, 'tok', 'head')
All inputs are finite; a program needn't handle non-finite values.
Results may differ from a plain program's by a relative error of at most 0.0085.
Values may be sent and summed in bfloat16 or wider, within the bound.
No kernel may reach another device: no remote copies, remote signals or barrier semaphores. Data moves between devices by JAX's collectives and lax.ppermute only.
A program may use at most 64 MiB of HBM per device.

v0:
```python
import jax
import jax.numpy as jnp
from jax import lax
from jax.sharding import PartitionSpec as P

HD = 128
GUIDE = 3.0


def combined_all(part, axis, combine):
    gathered = jax.tree.map(lambda a: lax.all_gather(a, axis), part)

    def take(source):
        return jax.tree.map(lambda a: lax.dynamic_index_in_dim(a, source, 0, False), gathered)

    return lax.fori_loop(
        1, lax.axis_size(axis), lambda source, state: combine(state, take(source)), take(0)
    )


def shifted(value, axis, steps):
    count = lax.axis_size(axis)
    leading, last = (max(0, -steps), min(count, count - steps))
    return lax.ppermute(value, axis, [(source, source + steps) for source in range(leading, last)])


def merge_stats(earlier, latter):
    row_top = jnp.maximum(earlier[0], latter[0])
    total_sum = earlier[1] * jnp.exp(earlier[0] - row_top) + latter[1] * jnp.exp(
        latter[0] - row_top
    )
    return (row_top, total_sum)


def body(
    held_cotangents,
    entering_adjoint,
    saved_queries,
    saved_keys,
    value_weight,
    out_weight,
    block_gate,
    time_gate,
    timestep,
):
    steps_index = jnp.arange(time_gate.shape[0])
    time_row = jnp.sum(
        jnp.where((steps_index == timestep[0])[:, None], time_gate, jnp.zeros_like(time_gate)),
        axis=0,
    )
    gate_row = block_gate[0] + time_row
    whole_cot = lax.all_gather(held_cotangents[0], "head", axis=2, tiled=True)
    scaled = (whole_cot.astype(jnp.float32) * gate_row).astype(jnp.bfloat16)
    out_full = lax.all_gather(out_weight[0], "tok", axis=0, tiled=True)
    attn_grad = jnp.einsum(
        "btd,dk->btk", scaled, out_full, preferred_element_type=jnp.float32
    ).astype(jnp.bfloat16)
    rows_here = saved_queries.shape[1]
    groups_here = saved_queries.shape[2] // HD
    score_scale = HD ** (-0.5)
    normal_grad = attn_grad[0]
    query_all = lax.all_gather(saved_queries[0], "tok", axis=0, tiled=True)
    total_rows = query_all.shape[0]
    shards = total_rows // rows_here
    key_heads = saved_keys[0].reshape(rows_here, groups_here, HD)
    scores = (
        jnp.einsum(
            "ihe,jhe->hij",
            query_all.reshape(total_rows, groups_here, HD),
            key_heads,
            preferred_element_type=jnp.float32,
        )
        * score_scale
    )
    row_top = jnp.max(scores, axis=2)
    partial_total = jnp.sum(jnp.exp(scores - row_top[:, :, None]), axis=2)
    top_all, total_all = combined_all((row_top, partial_total), "tok", merge_stats)
    log_total = top_all + jnp.log(total_all)
    weights = jnp.exp(scores - log_total[:, :, None]).astype(jnp.bfloat16)
    grad_all = lax.all_gather(normal_grad, "tok", axis=0, tiled=True)
    blocked = jnp.einsum(
        "hbij,bihe->bjhe",
        weights.reshape(groups_here, shards, rows_here, rows_here),
        grad_all.reshape(shards, rows_here, groups_here, HD),
        preferred_element_type=jnp.float32,
    )
    blocked = lax.optimization_barrier(blocked.astype(jnp.bfloat16))
    value_grad = (
        jnp.sum(blocked.astype(jnp.float32), axis=0)
        .reshape(rows_here, groups_here * HD)
        .astype(jnp.bfloat16)
    )
    stacked = jnp.stack([value_grad, attn_grad[1]])
    partial_back = jnp.einsum(
        "btk,dk->btd", stacked, value_weight[0], preferred_element_type=jnp.float32
    )
    back_sum = lax.psum_scatter(
        partial_back.astype(jnp.bfloat16), "head", scatter_dimension=2, tiled=True
    ).astype(jnp.float32)
    block_cot = (held_cotangents[0].astype(jnp.float32) + back_sum).astype(jnp.bfloat16)
    passed_on = shifted(block_cot, "section", -1)
    entering_full = entering_adjoint.astype(jnp.float32)
    fresh_rows = jnp.stack([(1.0 + GUIDE) * entering_full, -GUIDE * entering_full]).astype(
        jnp.bfloat16
    )
    is_last = lax.axis_index("section") == lax.axis_size("section") - 1
    return jnp.where(is_last, fresh_rows, passed_on)[None]


def solution(mesh):
    return jax.shard_map(
        body,
        mesh=mesh,
        in_specs=(
            P("section", None, "tok", "head"),
            P("tok", "head"),
            P("section", "tok", "head"),
            P("section", "tok", "head"),
            P("section", None, "head"),
            P("section", "tok", "head"),
            P("section", None),
            P(),
            P(),
        ),
        out_specs=P("section", None, "tok", "head"),
        check_vma=False,
    )
```

profile of v0, /device:TPU:0, one launch (start us, length us, event | category | flops | bytes accessed | tf_op | source)
XLA Modules:
  0.0 187.7 jit_solution(18396355772146746361)
XLA Ops:
  6.5 0.0 copy-start
  6.5 0.0 copy-start.3
  6.5 0.0 all-gather.11.cloned.1.call-start
  6.5 0.7 all-gather.11.cloned.1.call-update
  7.3 0.0 all-gather.13.cloned.1.call-start
  7.3 0.7 all-gather.13.cloned.1.call-update
  8.0 0.0 reduce-scatter.4.cloned.1.call-start
  8.7 1.7 copy.22
  10.4 1.1 copy.23
  11.5 0.0 copy-done.3
  11.6 1.1 select_reduce_fusion
  12.7 19.1 %all-gather.3 = bf16[1,512,640]{1,2,0:T(8,128)(2,1)S(1)} all-gather(bf16[1,128,640]{1,2,0:T(8,128)(2,1)} %copy.22), channel_id=5, replica_groups=mesh['section'=2,'head'=4,'tok'=4] {'tok'}, dimensions={1}, use_global_device_ids=true | all-gather | bytes 819200 | tf_op jit(solution)/shard_map/all_gather | solution.py:62
  31.7 0.6 fusion.28
  32.4 0.0 copy-start.1
  32.4 13.4 %all-gather.6 = f32[4,5,512]{2,1,0:T(8,128)S(1)} all-gather(f32[1,5,512]{2,1,0:T(8,128)S(1)} %bitcast.70), channel_id=6, replica_groups=mesh['section'=2,'head'=4,'tok'=4] {'tok'}, dimensions={0}, use_global_device_ids=true | all-gather | bytes 51200 | tf_op jit(solution)/shard_map/all_gather | solution.py:11
  45.8 0.0 copy-done.1
  45.8 0.8 exponential_reduce_fusion
  46.6 14.1 %all-gather.7 = f32[4,5,512]{2,1,0:T(8,128)S(1)} all-gather(f32[1,5,512]{2,1,0:T(8,128)S(1)} %bitcast.71), channel_id=7, replica_groups=mesh['section'=2,'head'=4,'tok'=4] {'tok'}, dimensions={0}, use_global_device_ids=true | all-gather | bytes 51200 | tf_op jit(solution)/shard_map/all_gather | solution.py:11
  60.7 0.1 while.17
  60.9 2.6 %exponential_convert_fusion = bf16[5,512,128]{2,1,0:T(8,128)(2,1)} fusion(f32[5,512,128]{2,1,0:T(8,128)} %copy-done.1, f32[5,512]{1,0:T(8,128)S(1)} %log_add_fusion), kind=kLoop, calls=%fused_computation.15 | loop fusion | flops 655360 | bytes 1976320 | tf_op jit(solution)/shard_map/convert_element_type | solution.py:79
  63.4 0.0 all-gather.11.cloned.1.call-done
  63.4 34.6 %all-gather.13.cloned.1.call-done = bf16[1,2560,640]{2,1,0:T(8,128)(2,1)} async-done(((bf16[1,640,640]{2,1,0:T(8,128)(2,1)}), bf16[1,2560,640]{2,1,0:T(8,128)(2,1)}) %all-gather.13.cloned.1.call-update) | async-done | bytes 3276816 | tf_op jit(solution)/shard_map/all_gather | solution.py:54
  98.0 3.5 %fusion.10 = bf16[2,128,640]{2,1,0:T(8,128)(2,1)S(1)} fusion(bf16[1,2560,640]{2,1,0:T(8,128)(2,1)} %all-gather.13.cloned.1.call-done, bf16[1,2,128,2560]{3,2,1,0:T(8,128)(2,1)} %all-gather.11.cloned.1.call-done, f32[2560]{0:T(1024)S(1)} %add.62), kind=kOutput, calls=%fused_computation.19 | convolution fusion | flops 840990720 | bytes 4925440 | tf_op jit(solution)/shard_map/btd,dk->btk/dot_general | solution.py:55
  101.6 0.7 fusion.27
  102.3 17.6 %all-gather.2 = bf16[1,512,640]{2,1,0:T(8,128)(2,1)} all-gather(bf16[1,128,640]{2,1,0:T(8,128)(2,1)S(1)} %get-tuple-element.152), channel_id=4, replica_groups=mesh['section'=2,'head'=4,'tok'=4] {'tok'}, dimensions={1}, use_global_device_ids=true | all-gather | bytes 819200 | tf_op jit(solution)/shard_map/all_gather | solution.py:80
  119.9 2.5 %reshape.61 = bf16[4,128,5,128]{3,2,1,0:T(8,128)(2,1)} reshape(bf16[1,512,640]{2,1,0:T(8,128)(2,1)} %all-gather.2) | data formatting | bytes 1310720 | tf_op jit(solution)/shard_map/reshape | solution.py:84
  122.4 2.7 %fusion.9 = bf16[4,128,5,128]{1,3,2,0:T(8,128)(2,1)} fusion(bf16[4,128,5,128]{3,2,1,0:T(8,128)(2,1)} %reshape.61, bf16[5,4,128,128]{3,2,1,0:T(8,128)(2,1)} %bitcast.66), kind=kOutput, calls=%fused_computation.18 | convolution fusion | flops 84213760 | bytes 1966080 | tf_op jit(solution)/shard_map/hbij,bihe->bjhe/dot_general | solution.py:81
  125.1 1.2 reduce_sum.32
  126.3 0.8 copy.28
  127.1 0.0 copy-done
  127.1 3.3 %convolution_convert_fusion = bf16[2,128,2560]{2,1,0:T(8,128)(2,1)} fusion(bf16[1,2560,640]{2,1,0:T(8,128)(2,1)S(1)} %copy-done, bf16[1,128,640]{2,1,0:T(8,128)(2,1)} %get-tuple-element.153, bf16[1,128,640]{2,1,0:T(8,128)(2,1)} %copy.28), kind=kOutput, calls=%fused_computation.5 | convolution fusion | flops 839680000 | bytes 4915200 | tf_op jit(solution)/shard_map/btk,dk->btd/dot_general | solution.py:94
  130.4 4.3 %copy.33 = bf16[2,128,2560]{1,0,2:T(2,128)(2,1)} copy(bf16[2,128,2560]{2,1,0:T(8,128)(2,1)} %convolution_convert_fusion) | data formatting | bytes 2621440
  134.7 2.6 %copy.41 = bf16[320,8,2,128]{3,1,2,0:T(8,128)(2,1)} copy(bf16[320,8,2,128]{3,2,1,0:T(2,128)(2,1)} %bitcast.64) | data formatting | bytes 2621440
  137.2 0.0 reduce-scatter.4.cloned.1.call-update
  137.3 0.0 copy-start.2
  137.3 25.1 %reduce-scatter.4.cloned.1.call-done = bf16[640,256]{1,0:T(8,128)(2,1)} async-done(((bf16[2560,256]{1,0:T(8,128)(2,1)}), bf16[640,256]{1,0:T(8,128)(2,1)}) %reduce-scatter.4.cloned.1.call-update) | async-done | bytes 327696
  162.4 1.8 reshape.63
  164.1 1.9 %copy.34 = bf16[2,128,640]{2,1,0:T(8,128)(2,1)} copy(bf16[2,128,640]{1,0,2:T(2,128)(2,1)} %bitcast.67) | data formatting | bytes 655360
  166.1 1.9 fusion.15
  167.9 1.3 collective-permute-start
  169.2 0.0 copy-done.2
  169.3 10.1 %collective-permute-done = bf16[2,128,640]{2,1,0:T(8,128)(2,1)} collective-permute-done((bf16[2,128,640]{2,1,0:T(8,128)(2,1)}, bf16[2,128,640]{2,1,0:T(8,128)(2,1)}, u32[]{:S(2)}, u32[]{:S(2)}) %collective-permute-start) | collective-permute-done | bytes 327712 | tf_op jit(solution)/shard_map/ppermute | solution.py:24
  179.4 1.7 fusion.20
  (10 shorter events, 0.2 us)
Async XLA Ops:
  6.5 120.6 %copy-start = (bf16[1,2560,640]{2,1,0:T(8,128)(2,1)S(1)}, bf16[1,2560,640]{2,1,0:T(8,128)(2,1)}, u32[]{:S(2)}) copy-start(bf16[1,2560,640]{2,1,0:T(8,128)(2,1)} %param.15) | copy-start | bytes 9830404
  6.5 5.0 %copy-start.3 = (f32[1,2560]{1,0:T(1,128)S(1)}, f32[1,2560]{1,0:T(1,128)}, u32[]{:S(2)}) copy-start(f32[1,2560]{1,0:T(1,128)} %param.17) | copy-start | bytes 30724
  6.5 56.9 %all-gather.11.cloned.1.call-start = ((), (), s32[]{:S(2)}) async-start(), calls=%async_computation.1 | async-start | bytes 1638400 | tf_op jit(solution)/shard_map/all_gather | solution.py:52
  7.3 90.8 %all-gather.13.cloned.1.call-start = ((), (), s32[]{:S(2)}) async-start(), calls=%async_computation.2 | async-start | bytes 4096000 | tf_op jit(solution)/shard_map/all_gather | solution.py:54
  8.0 154.4 %reduce-scatter.4.cloned.1.call-start = ((), (), s32[]{:S(2)}) async-start(), calls=%async_computation.3 | async-start | bytes 1638400
  32.4 13.4 %copy-start.1 = (f32[5,512,128]{2,1,0:T(8,128)}, f32[5,512,128]{2,1,0:T(8,128)S(1)}, u32[]{:S(2)}) copy-start(f32[5,512,128]{2,1,0:T(8,128)S(1)} %get-tuple-element.157) | copy-start | bytes 3932164
  137.3 32.0 %copy-start.2 = (bf16[128,640]{1,0:T(8,128)(2,1)S(1)}, bf16[128,640]{1,0:T(8,128)(2,1)}, u32[]{:S(2)}) copy-start(bf16[128,640]{1,0:T(8,128)(2,1)} %param.12) | copy-start | bytes 491524
  167.9 11.5 %collective-permute-start = (bf16[2,128,640]{2,1,0:T(8,128)(2,1)}, bf16[2,128,640]{2,1,0:T(8,128)(2,1)}, u32[]{:S(2)}, u32[]{:S(2)}) collective-permute-start(bf16[2,128,640]{2,1,0:T(8,128)(2,1)} %fusion.15), channel_id=1, source_target_pairs={{16,0},{17,1},{18,2},{19,3},{20,4},{21,5},{22,6},{23,7},{24,8},{25... | collective-permute-start | bytes 983048 | tf_op jit(solution)/shard_map/ppermute | solution.py:24
Sparse Core Ops, SparseCore 0:
  8.9 20.8 all-gather.10
  31.4 66.6 all-gather.12
  137.4 24.9 reduce-scatter.3
where the time goes:
time: 188 us
  waiting for transfers between devices  71.2 us (38%)
  blocking collectives  64.3 us (34%)
  local copies, waits for them, and re-layouts  17.4 us (9%)
  between operations  13.9 us (7%)
  matrix products  10.1 us (5%)
  other arithmetic  9.44 us (5%)
    all_gather x1, waiting for transfers between devices, body(): out_full = lax.all_gather(out_weight[0], 'tok', axis=0, tiled=True)  34.6 us
    all_gather x2, blocking collectives, combined_all(): gathered = jax.tree.map(lambda a: lax.all_gather(a, axis), part)  27.5 us
    unnamed x4, waiting for transfers between devices  26.5 us
    all_gather x1, blocking collectives, body(): query_all = lax.all_gather(saved_queries[0], 'tok', axis=0, tiled=True)  19.1 us
    all_gather x1, blocking collectives, body(): grad_all = lax.all_gather(normal_grad, 'tok', axis=0, tiled=True)  17.6 us
    unnamed x14, local copies, waits for them, and re-layouts  13.3 us
    ppermute x1, waiting for transfers between devices, shifted(): lax.ppermute(value, axis, [(source, source + steps) for source in range(l...  10.1 us
  transfers between devices with their start and end apart: 4, of which 3 were waited for; matrix products, arithmetic and copies ran while one was open for 4% of the time, Pallas kernels for 0%

commit v1 on v0

--- a/solution.py
+++ b/solution.py
@@ -2,9 +2,25 @@
 import jax.numpy as jnp
 from jax import lax
 from jax.sharding import PartitionSpec as P
+from jax.lax import axis_index, ppermute, psum
 
 HD = 128
 GUIDE = 3.0
+
+
+def list_shapes(inputs, mat):
+    device_axis = "tok"
+    piece_now, known, d_next = (psum(1, device_axis), axis_index(device_axis), inputs.shape[0])
+    tray = list(map(lambda j: (j, (j + 1) % piece_now), range(piece_now)))
+    raw_out, v_now = (inputs, None)
+    i = 0
+    while i < piece_now:
+        built = ppermute(raw_out, device_axis, tray) if i < piece_now - 1 else None
+        latest = mat(raw_out, (known - i) % piece_now * d_next)
+        v_now = latest if v_now is None else v_now + latest
+        raw_out = built
+        i += 1
+    return v_now
 
 
 def combined_all(part, axis, combine):
@@ -51,9 +67,14 @@
     gate_row = block_gate[0] + time_row
     whole_cot = lax.all_gather(held_cotangents[0], "head", axis=2, tiled=True)
     scaled = (whole_cot.astype(jnp.float32) * gate_row).astype(jnp.bfloat16)
-    out_full = lax.all_gather(out_weight[0], "tok", axis=0, tiled=True)
-    attn_grad = jnp.einsum(
-        "btd,dk->btk", scaled, out_full, preferred_element_type=jnp.float32
+    attn_grad = list_shapes(
+        out_weight[0],
+        lambda part_2, start: jnp.einsum(
+            "btd,dk->btk",
+            lax.dynamic_slice_in_dim(scaled, start, part_2.shape[0], axis=2),
+            part_2,
+            preferred_element_type=jnp.float32,
+        ),
     ).astype(jnp.bfloat16)
     rows_here = saved_queries.shape[1]
     groups_here = saved_queries.shape[2] // HD

time: 188 us -> 198 us (1.053)
  blocking collectives: 64.3 us -> 74.1 us
  waiting for transfers between devices: 71.2 us -> 62.7 us
  starting transfers between devices: 1.36 us -> 4.49 us
  matrix products: 10.1 us -> 13 us
    all_gather x1 -> x0, waiting for transfers between devices: 34.6 us -> none  [body(): out_full = lax.all_gather(out_weight[0], 'tok', axis=0, tiled=True)]
    ppermute x0 -> x3, waiting for transfers between devices: none -> 26.9 us  [list_shapes(): built = ppermute(raw_out, device_axis, tray) if i < piece_now - 1 else None]
    all_gather x1, blocking collectives: 19.1 us -> 31.7 us  [body(): query_all = lax.all_gather(saved_queries[0], 'tok', axis=0, tiled=True)]
    ppermute x0 -> x3, starting transfers between devices: none -> 3.17 us  [list_shapes(): built = ppermute(raw_out, device_axis, tray) if i < piece_now - 1 else None]
    dot_general x1 -> x4, matrix products: 3.51 us -> 5.27 us  [body(): jnp.einsum('btd,dk->btk', lax.dynamic_slice_in_dim(scaled, start, part_2....]
    unnamed x4 -> x3, waiting for transfers between devices: 26.5 us -> 25.7 us
    unnamed x14 -> x16, local copies, waits for them, and re-layouts: 13.3 us -> 13.8 us
  transfers between devices with their start and end apart: 4 -> 6, of which waited for: 3 -> 4; matrix products, arithmetic and copies ran while one was open for 4% -> 7% of each run, Pallas kernels for 0% -> 0%
where the time goes in v1:
time: 198 us
  blocking collectives  74.1 us (37%)
  waiting for transfers between devices  62.7 us (32%)
  local copies, waits for them, and re-layouts  17.8 us (9%)
  between operations  14.3 us (7%)
  matrix products  13 us (7%)
  other arithmetic  11 us (6%)
  starting transfers between devices  4.49 us (2%)
    all_gather x1, blocking collectives, body(): query_all = lax.all_gather(saved_queries[0], 'tok', axis=0, tiled=True)  31.7 us
    ppermute x3, waiting for transfers between devices, list_shapes(): built = ppermute(raw_out, device_axis, tray) if i < piece_now - 1 else None  26.9 us
    all_gather x2, blocking collectives, combined_all(): gathered = jax.tree.map(lambda a: lax.all_gather(a, axis), part)  26.5 us
    unnamed x3, waiting for transfers between devices  25.7 us
    all_gather x1, blocking collectives, body(): grad_all = lax.all_gather(normal_grad, 'tok', axis=0, tiled=True)  16 us
    unnamed x16, local copies, waits for them, and re-layouts  13.8 us
    ppermute x1, waiting for transfers between devices, shifted(): lax.ppermute(value, axis, [(source, source + steps) for source in range(l...  10.1 us
    dot_general x4, matrix products, body(): jnp.einsum('btd,dk->btk', lax.dynamic_slice_in_dim(scaled, start, part_2....  5.27 us
  transfers between devices with their start and end apart: 6, of which 4 were waited for; matrix products, arithmetic and copies ran while one was open for 7% of the time, Pallas kernels for 0%

profile of v1, /device:TPU:0, one launch (start us, length us, event | category | flops | bytes accessed | tf_op | source)
XLA Modules:
  0.0 197.6 jit_solution(10782131385652167420)
XLA Ops:
  6.5 0.0 copy-start
  6.5 0.0 all-gather.9.cloned.1.call-start
  6.5 0.7 all-gather.9.cloned.1.call-update
  7.3 0.0 reduce-scatter.4.cloned.1.call-start
  7.3 3.1 %collective-permute-start = (bf16[640,640]{1,0:T(8,128)(2,1)}, bf16[640,640]{1,0:T(8,128)(2,1)}, u32[]{:S(2)}, u32[]{:S(2)}) collective-permute-start(bf16[640,640]{1,0:T(8,128)(2,1)} %bitcast.70), channel_id=1, source_target_pairs={{0,1},{1,2},{2,3},{3,0},{4,5},{5,6},{6,7},{7,4},{8,9},{9,10},{10,1... | collective-permute-start | bytes 2457608 | tf_op jit(solution)/shard_map/ppermute | solution.py:18
  10.4 1.1 copy.22
  11.5 31.7 %all-gather.2 = bf16[1,512,640]{1,2,0:T(8,128)(2,1)} all-gather(bf16[1,128,640]{1,2,0:T(8,128)(2,1)S(1)} %copy.22), channel_id=4, replica_groups=mesh['section'=2,'head'=4,'tok'=4] {'tok'}, dimensions={1}, use_global_device_ids=true | all-gather | bytes 819200 | tf_op jit(solution)/shard_map/all_gather | solution.py:83
  43.2 1.1 copy.23
  44.3 1.7 fusion.32
  46.0 0.0 copy-start.4
  46.0 1.1 copy-done.1
  47.1 0.8 exponential_reduce_fusion
  47.9 13.1 %all-gather.5 = f32[4,5,512]{2,1,0:T(8,128)S(1)} all-gather(f32[1,5,512]{2,1,0:T(8,128)S(1)} %bitcast.73), channel_id=5, replica_groups=mesh['section'=2,'head'=4,'tok'=4] {'tok'}, dimensions={0}, use_global_device_ids=true | all-gather | bytes 51200 | tf_op jit(solution)/shard_map/all_gather | solution.py:27
  61.0 13.3 %all-gather.6 = f32[4,5,512]{2,1,0:T(8,128)S(1)} all-gather(f32[1,5,512]{2,1,0:T(8,128)S(1)} %bitcast.74), channel_id=6, replica_groups=mesh['section'=2,'head'=4,'tok'=4] {'tok'}, dimensions={0}, use_global_device_ids=true | all-gather | bytes 51200 | tf_op jit(solution)/shard_map/all_gather | solution.py:27
  74.3 0.0 collective-permute-done
  74.3 0.1 collective-permute-start.1
  74.4 0.1 while.17
  75.3 0.0 copy-done.4
  75.3 1.1 select_reduce_fusion
  76.5 2.6 %exponential_convert_fusion = bf16[5,512,128]{2,1,0:T(8,128)(2,1)} fusion(f32[5,512,128]{2,1,0:T(8,128)} %copy-done.1, f32[5,512]{1,0:T(8,128)S(1)} %log_add_fusion), kind=kLoop, calls=%fused_computation.12 | loop fusion | flops 655360 | bytes 1976320 | tf_op jit(solution)/shard_map/convert_element_type | solution.py:100
  79.1 14.5 %collective-permute-done.1 = bf16[640,640]{1,0:T(8,128)(2,1)} collective-permute-done((bf16[640,640]{1,0:T(8,128)(2,1)}, bf16[640,640]{1,0:T(8,128)(2,1)}, u32[]{:S(2)}, u32[]{:S(2)}) %collective-permute-start.1) | collective-permute-done | bytes 819232 | tf_op jit(solution)/shard_map/ppermute | solution.py:18
  93.6 0.0 collective-permute-start.2
  93.6 1.6 fusion.3
  95.2 0.0 copy-done.2
  95.2 0.5 fusion.9
  95.7 1.6 convolution_add_fusion.2
  97.3 1.6 convolution_add_fusion.1
  98.9 12.4 %collective-permute-done.2 = bf16[640,640]{1,0:T(8,128)(2,1)} collective-permute-done((bf16[640,640]{1,0:T(8,128)(2,1)}, bf16[640,640]{1,0:T(8,128)(2,1)}, u32[]{:S(2)}, u32[]{:S(2)}) %collective-permute-start.2) | collective-permute-done | bytes 819232 | tf_op jit(solution)/shard_map/ppermute | solution.py:18
  111.2 1.6 fusion.5
  112.9 0.7 fusion.31
  113.5 16.0 %all-gather.1 = bf16[1,512,640]{2,1,0:T(8,128)(2,1)} all-gather(bf16[1,128,640]{2,1,0:T(8,128)(2,1)S(1)} %get-tuple-element.152), channel_id=3, replica_groups=mesh['section'=2,'head'=4,'tok'=4] {'tok'}, dimensions={1}, use_global_device_ids=true | all-gather | bytes 819200 | tf_op jit(solution)/shard_map/all_gather | solution.py:101
  129.5 2.5 %reshape.63 = bf16[4,128,5,128]{3,2,1,0:T(8,128)(2,1)} reshape(bf16[1,512,640]{2,1,0:T(8,128)(2,1)} %all-gather.1) | data formatting | bytes 1310720 | tf_op jit(solution)/shard_map/reshape | solution.py:105
  132.1 2.7 %fusion.4 = bf16[4,128,5,128]{1,3,2,0:T(8,128)(2,1)} fusion(bf16[4,128,5,128]{3,2,1,0:T(8,128)(2,1)} %reshape.63, bf16[5,4,128,128]{3,2,1,0:T(8,128)(2,1)} %bitcast.68), kind=kOutput, calls=%fused_computation.14 | convolution fusion | flops 84213760 | bytes 1966080 | tf_op jit(solution)/shard_map/hbij,bihe->bjhe/dot_general | solution.py:102
  134.7 1.2 reduce_sum.32
  136.0 0.8 copy.28
  136.8 0.0 copy-done
  136.8 3.3 %convolution_convert_fusion = bf16[2,128,2560]{2,1,0:T(8,128)(2,1)} fusion(bf16[1,2560,640]{2,1,0:T(8,128)(2,1)S(1)} %copy-done, bf16[1,128,640]{2,1,0:T(8,128)(2,1)} %get-tuple-element.153, bf16[1,128,640]{2,1,0:T(8,128)(2,1)} %copy.28), kind=kOutput, calls=%fused_computation.5 | convolution fusion | flops 839680000 | bytes 4915200 | tf_op jit(solution)/shard_map/btk,dk->btd/dot_general | solution.py:115
  140.1 4.3 %copy.33 = bf16[2,128,2560]{1,0,2:T(2,128)(2,1)} copy(bf16[2,128,2560]{2,1,0:T(8,128)(2,1)} %convolution_convert_fusion) | data formatting | bytes 2621440
  144.3 2.5 %copy.41 = bf16[320,8,2,128]{3,1,2,0:T(8,128)(2,1)} copy(bf16[320,8,2,128]{3,2,1,0:T(2,128)(2,1)} %bitcast.66) | data formatting | bytes 2621440
  146.9 0.0 reduce-scatter.4.cloned.1.call-update
  146.9 0.0 copy-start.3
  146.9 25.0 %reduce-scatter.4.cloned.1.call-done = bf16[640,256]{1,0:T(8,128)(2,1)} async-done(((bf16[2560,256]{1,0:T(8,128)(2,1)}), bf16[640,256]{1,0:T(8,128)(2,1)}) %reduce-scatter.4.cloned.1.call-update) | async-done | bytes 327696
  171.9 1.8 reshape.65
  173.7 1.9 copy.34
  175.6 1.9 fusion.11
  177.5 1.3 collective-permute-start.3
  178.9 10.1 %collective-permute-done.3 = bf16[2,128,640]{2,1,0:T(8,128)(2,1)} collective-permute-done((bf16[2,128,640]{2,1,0:T(8,128)(2,1)}, bf16[2,128,640]{2,1,0:T(8,128)(2,1)}, u32[]{:S(2)}, u32[]{:S(2)}) %collective-permute-start.3) | collective-permute-done | bytes 327712 | tf_op jit(solution)/shard_map/ppermute | solution.py:40
  189.0 1.7 fusion.16
  (14 shorter events, 0.2 us)
Async XLA Ops:
  6.5 130.3 %copy-start = (bf16[1,2560,640]{2,1,0:T(8,128)(2,1)S(1)}, bf16[1,2560,640]{2,1,0:T(8,128)(2,1)}, u32[]{:S(2)}) copy-start(bf16[1,2560,640]{2,1,0:T(8,128)(2,1)} %param.15) | copy-start | bytes 9830404
  6.5 87.0 %all-gather.9.cloned.1.call-start = ((), (), s32[]{:S(2)}) async-start(), calls=%async_computation.1 | async-start | bytes 1638400 | tf_op jit(solution)/shard_map/all_gather | solution.py:68
  7.3 164.7 %reduce-scatter.4.cloned.1.call-start = ((), (), s32[]{:S(2)}) async-start(), calls=%async_computation.2 | async-start | bytes 1638400
  7.3 67.0 %collective-permute-start = (bf16[640,640]{1,0:T(8,128)(2,1)}, bf16[640,640]{1,0:T(8,128)(2,1)}, u32[]{:S(2)}, u32[]{:S(2)}) collective-permute-start(bf16[640,640]{1,0:T(8,128)(2,1)} %bitcast.70), channel_id=1, source_target_pairs={{0,1},{1,2},{2,3},{3,0},{4,5},{5,6},{6,7},{7,4},{8,9},{9,10},{10,1... | collective-permute-start | bytes 2457608 | tf_op jit(solution)/shard_map/ppermute | solution.py:18
  46.0 1.1 copy-start.1
  46.0 29.3 %copy-start.4 = (f32[1,2560]{1,0:T(1,128)S(1)}, f32[1,2560]{1,0:T(1,128)}, u32[]{:S(2)}) copy-start(f32[1,2560]{1,0:T(1,128)} %param.17) | copy-start | bytes 30724
  74.3 19.2 %collective-permute-start.1 = (bf16[640,640]{1,0:T(8,128)(2,1)}, bf16[640,640]{1,0:T(8,128)(2,1)}, u32[]{:S(2)}, u32[]{:S(2)}) collective-permute-start(bf16[640,640]{1,0:T(8,128)(2,1)} %collective-permute-done), channel_id=1, source_target_pairs={{0,1},{1,2},{2,3},{3,0},{4,5},{5,6},{6,7},{7,4},{8,9},{9,10},{10,1... | collective-permute-start | bytes 2457608 | tf_op jit(solution)/shard_map/ppermute | solution.py:18
  93.6 17.7 %collective-permute-start.2 = (bf16[640,640]{1,0:T(8,128)(2,1)}, bf16[640,640]{1,0:T(8,128)(2,1)}, u32[]{:S(2)}, u32[]{:S(2)}) collective-permute-start(bf16[640,640]{1,0:T(8,128)(2,1)} %collective-permute-done.1), channel_id=1, source_target_pairs={{0,1},{1,2},{2,3},{3,0},{4,5},{5,6},{6,7},{7,4},{8,9},{9,10},{10,1... | collective-permute-start | bytes 2457608 | tf_op jit(solution)/shard_map/ppermute | solution.py:18
  93.6 1.6 copy-start.2
  146.9 31.9 %copy-start.3 = (bf16[128,640]{1,0:T(8,128)(2,1)S(1)}, bf16[128,640]{1,0:T(8,128)(2,1)}, u32[]{:S(2)}) copy-start(bf16[128,640]{1,0:T(8,128)(2,1)} %param.12) | copy-start | bytes 491524
  177.5 11.5 %collective-permute-start.3 = (bf16[2,128,640]{2,1,0:T(8,128)(2,1)}, bf16[2,128,640]{2,1,0:T(8,128)(2,1)}, u32[]{:S(2)}, u32[]{:S(2)}) collective-permute-start(bf16[2,128,640]{2,1,0:T(8,128)(2,1)} %fusion.11), channel_id=1, source_target_pairs={{16,0},{17,1},{18,2},{19,3},{20,4},{21,5},{22,6},{23,7},{24,8},{25... | collective-permute-start | bytes 983048 | tf_op jit(solution)/shard_map/ppermute | solution.py:40
Sparse Core Ops, SparseCore 0:
  8.9 20.8 all-gather.8
  147.0 24.8 reduce-scatter.3
